TPU v7x, 32 devices: a whole 2x2x4 slice. The times are simulated.
32 devices in a mesh: rows: 4 (over y, x), pairs: 8 (over z, core).
Axes of the slice: x: 2, y: 2, z: 4, core: 2. Of those that a mesh axis runs over, the one named last changes fastest.
Arguments:
- latent: bfloat16 [8192, 3072], P('rows', 'pairs'), as said below
Outputs:
- rotated_latent: bfloat16 [8192, 3072], P('rows', 'pairs')
Inputs may be any that keep to these rules, and one draw needn't show every extreme that they name: `latent`: finite real entries.
All inputs are finite; a program needn't handle non-finite values.
Results may differ from a plain program's by a relative error of at most 0.0065.
Values may be sent and summed in bfloat16 or wider, within the bound.
No kernel may reach another device: no remote copies, remote signals or barrier semaphores. Data moves between devices by JAX's collectives and lax.ppermute only.
A program may use at most 64 MiB of HBM per device.

v0:
```python
import math
import jax
import jax.numpy as jnp
from jax import lax
from jax.sharding import PartitionSpec as P

ROUNDS = 2
NS_ITERS = 2


def passed_along(shard, axis, by):
    peers = lax.axis_size(axis)
    return lax.ppermute(shard, axis, [(i, (i + by) % peers) for i in range(peers)])


def orthogonal(norms, cross):
    half = cross.shape[0]
    corr = cross / jnp.sqrt(norms[:half, None] * norms[None, half:])
    total = jnp.sqrt(2.0 * jnp.sum(corr * corr) + 1e-12)
    scaled = corr * (8.0 / total)
    empty = jnp.zeros((half, half), jnp.float32)
    upper = jnp.concatenate([empty, scaled], axis=1)
    lower = jnp.concatenate([-scaled.T, empty], axis=1)
    ident = jnp.eye(2 * half, dtype=jnp.float32)
    current = (ident + jnp.concatenate([upper, lower], axis=0)) * (1.5 / math.sqrt(65.0))
    for _ in range(NS_ITERS):
        inner = jnp.dot(current.T, current, precision=lax.Precision.HIGHEST)
        current = 1.5 * current - 0.5 * jnp.dot(current, inner, precision=lax.Precision.HIGHEST)
    return current.astype(jnp.bfloat16)


def rotor_of(window):
    half = window.shape[1] // 2
    gram = jnp.dot(window.T, window, preferred_element_type=jnp.float32)
    gram = lax.psum(gram, "rows")
    return orthogonal(jnp.diagonal(gram), gram[:half, half:])


def local(latent):
    half = latent.shape[1] // 2
    window = latent
    for _ in range(ROUNDS):
        from_below = passed_along(window, "pairs", 1)
        from_above = passed_along(window, "pairs", -1)
        rotor = rotor_of(window)
        left_rotor = passed_along(rotor[:, :half], "pairs", 1)
        right_rotor = passed_along(rotor[:, half:], "pairs", -1)
        left_next = jnp.dot(from_below, left_rotor, preferred_element_type=jnp.float32).astype(
            jnp.bfloat16
        )
        right_next = jnp.dot(from_above, right_rotor, preferred_element_type=jnp.float32).astype(
            jnp.bfloat16
        )
        window = jnp.concatenate([left_next, right_next], axis=1)
    return window


def solution(mesh):
    return jax.shard_map(
        local,
        mesh=mesh,
        in_specs=(P("rows", "pairs"),),
        out_specs=P("rows", "pairs"),
        check_vma=False,
    )
```

profile of v0, /device:TPU:0, one launch (start us, length us, event | category | flops | bytes accessed | tf_op | source)
XLA Modules:
  0.0 162.5 jit_solution(6450090133549089609)
XLA Ops:
  6.5 3.9 %fusion.51 = f32[384,384]{1,0:T(8,128)} fusion(bf16[2048,384]{1,0:T(8,128)(2,1)} %param.1), kind=kOutput, calls=%fused_computation.75 | convolution fusion | flops 603979776 | bytes 2162688 | tf_op jit(solution)/shard_map/dot_general | solution.py:34
  10.5 4.6 %collective-permute-start.3 = (bf16[2048,384]{1,0:T(8,128)(2,1)S(1)}, bf16[2048,384]{1,0:T(8,128)(2,1)}, u32[]{:S(2)}, u32[]{:S(2)}) collective-permute-start(bf16[2048,384]{1,0:T(8,128)(2,1)S(1)} %copy-done.2), channel_id=1, source_target_pairs={{0,7},{1,0},{2,1},{3,2},{4,3},{5,4},{6,5},{7,6},{8,15},{9,8},{10,9... | collective-permute-start | bytes 4718600 | tf_op jit(solution)/shard_map/ppermute | solution.py:13
  15.1 44.2 %all-reduce.7.cloned.1.call-done = f32[384,384]{1,0:T(8,128)} async-done(((f32[384,384]{1,0:T(8,128)}), f32[384,384]{1,0:T(8,128)}) %all-reduce.7.cloned.1.call-update) | async-done | bytes 589840 | tf_op jit(solution)/shard_map/psum | solution.py:35
  59.3 6.3 %gather_fusion = f32[384]{0:T(512)S(1)} fusion(f32[384,384]{1,0:T(8,128)} %all-reduce.7.cloned.1.call-done, s32[384]{0:T(512)S(1)} %or_reduce_fusion), kind=kCustom, calls=%fused_computation | custom fusion | bytes 6144 | tf_op jit(solution)/shard_map/jit(diagonal)/cond/branch_0_fun/gather | solution.py:36
  67.4 1.3 fusion.12
  68.7 1.4 fusion.2
  71.5 1.4 fusion.7
  72.9 2.6 %collective-permute-start.2 = (bf16[384,192]{0,1:T(8,128)(2,1)S(1)}, bf16[384,192]{0,1:T(8,128)(2,1)S(1)}, u32[]{:S(2)}, u32[]{:S(2)}) collective-permute-start(bf16[384,192]{0,1:T(8,128)(2,1)S(1)} %get-tuple-element.12), channel_id=1, source_target_pairs={{0,7},{1,0},{2,1},{3,2},{4,3},{5,4},{6,5},{7,6},{8,15},{9,8},{10,9... | collective-permute-start | bytes 442376 | tf_op jit(solution)/shard_map/ppermute | solution.py:13
  75.4 2.7 %collective-permute-done.2 = bf16[384,192]{0,1:T(8,128)(2,1)S(1)} collective-permute-done((bf16[384,192]{0,1:T(8,128)(2,1)S(1)}, bf16[384,192]{0,1:T(8,128)(2,1)S(1)}, u32[]{:S(2)}, u32[]{:S(2)}) %collective-permute-start.2) | collective-permute-done | bytes 147488 | tf_op jit(solution)/shard_map/ppermute | solution.py:13
  78.1 2.1 %fusion.1 = bf16[2048,192]{0,1:T(8,128)(2,1)S(1)} fusion(bf16[384,192]{0,1:T(8,128)(2,1)S(1)} %collective-permute-done.2, bf16[2048,384]{1,0:T(8,128)(2,1)} %collective-permute-done.3), kind=kOutput, calls=%fused_computation.7 | convolution fusion | flops 302383104 | bytes 2506752 | tf_op jit(solution)/shard_map/dot_general | solution.py:51
  80.3 1.5 collective-permute-done
  81.8 2.1 %fusion = bf16[2048,192]{0,1:T(8,128)(2,1)S(1)} fusion(bf16[384,192]{0,1:T(8,128)(2,1)S(1)} %collective-permute-done, bf16[2048,384]{1,0:T(8,128)(2,1)} %collective-permute-done.1), kind=kOutput, calls=%fused_computation.6 | convolution fusion | flops 302383104 | bytes 2506752 | tf_op jit(solution)/shard_map/dot_general | solution.py:48
  83.9 1.8 %fusion.44 = f32[384,384]{1,0:T(8,128)} fusion(bf16[2048,192]{0,1:T(8,128)(2,1)S(1)} %fusion.1, bf16[2048,192]{0,1:T(8,128)(2,1)S(1)} %fusion), kind=kOutput, calls=%fused_computation.70 | convolution fusion | flops 607125504 | bytes 2162688 | tf_op jit(solution)/shard_map/dot_general | solution.py:34
  87.0 2.2 %collective-permute-start.6 = (bf16[2048,384]{0,1:T(8,128)(2,1)}, bf16[2048,384]{0,1:T(8,128)(2,1)}, u32[]{:S(2)}, u32[]{:S(2)}) collective-permute-start(bf16[2048,384]{0,1:T(8,128)(2,1)} %pad_maximum_fusion), channel_id=1, source_target_pairs={{0,7},{1,0},{2,1},{3,2},{4,3},{5,4},{6,5},{7,6},{8,15},{9,8},{10,9... | collective-permute-start | bytes 4718600 | tf_op jit(solution)/shard_map/ppermute | solution.py:13
  89.3 41.6 %all-reduce.9.cloned.1.call-done = f32[384,384]{1,0:T(8,128)} async-done(((f32[384,384]{1,0:T(8,128)}), f32[384,384]{1,0:T(8,128)}) %all-reduce.9.cloned.1.call-update) | async-done | bytes 589840 | tf_op jit(solution)/shard_map/psum | solution.py:35
  130.9 6.3 %gather_fusion.1 = f32[384]{0:T(512)S(1)} fusion(f32[384,384]{1,0:T(8,128)} %all-reduce.9.cloned.1.call-done, s32[384]{0:T(512)S(1)} %or_reduce_fusion), kind=kCustom, calls=%fused_computation.1 | custom fusion | bytes 6144 | tf_op jit(solution)/shard_map/jit(diagonal)/cond/branch_0_fun/gather | solution.py:36
  139.0 1.3 fusion.9
  140.4 1.4 fusion.4
  143.1 1.3 fusion.6
  144.4 2.6 %collective-permute-start.7 = (bf16[384,192]{0,1:T(8,128)(2,1)S(1)}, bf16[384,192]{0,1:T(8,128)(2,1)S(1)}, u32[]{:S(2)}, u32[]{:S(2)}) collective-permute-start(bf16[384,192]{0,1:T(8,128)(2,1)S(1)} %get-tuple-element.10), channel_id=1, source_target_pairs={{0,7},{1,0},{2,1},{3,2},{4,3},{5,4},{6,5},{7,6},{8,15},{9,8},{10,9... | collective-permute-start | bytes 442376 | tf_op jit(solution)/shard_map/ppermute | solution.py:13
  147.0 2.7 %collective-permute-done.7 = bf16[384,192]{0,1:T(8,128)(2,1)S(1)} collective-permute-done((bf16[384,192]{0,1:T(8,128)(2,1)S(1)}, bf16[384,192]{0,1:T(8,128)(2,1)S(1)}, u32[]{:S(2)}, u32[]{:S(2)}) %collective-permute-start.7) | collective-permute-done | bytes 147488 | tf_op jit(solution)/shard_map/ppermute | solution.py:13
  149.7 2.0 %convolution_convert_fusion = bf16[2048,192]{0,1:T(8,128)(2,1)S(1)} fusion(bf16[384,192]{0,1:T(8,128)(2,1)S(1)} %collective-permute-done.7, bf16[2048,384]{0,1:T(8,128)(2,1)} %collective-permute-done.6), kind=kOutput, calls=%fused_computation.2 | convolution fusion | flops 302383104 | bytes 2506752 | tf_op jit(solution)/shard_map/dot_general | solution.py:51
  151.7 1.7 %collective-permute-done.5 = bf16[384,192]{0,1:T(8,128)(2,1)S(1)} collective-permute-done((bf16[384,192]{0,1:T(8,128)(2,1)S(1)}, bf16[384,192]{0,1:T(8,128)(2,1)S(1)}, u32[]{:S(2)}, u32[]{:S(2)}) %collective-permute-start.5) | collective-permute-done | bytes 147488 | tf_op jit(solution)/shard_map/ppermute | solution.py:13
  154.1 1.6 copy.7
  (34 shorter events, 6.9 us)
Async XLA Ops:
  6.5 4.0 %copy-start.2 = (bf16[2048,384]{1,0:T(8,128)(2,1)S(1)}, bf16[2048,384]{1,0:T(8,128)(2,1)}, u32[]{:S(2)}) copy-start(bf16[2048,384]{1,0:T(8,128)(2,1)} %param.1) | copy-start | bytes 4718596
  6.5 52.8 %all-reduce.7.cloned.1.call-start = ((), (), s32[]{:S(2)}) async-start(), calls=%async_computation | async-start | bytes 1179648 | tf_op jit(solution)/shard_map/psum | solution.py:35
  10.5 120.4 %all-reduce.9.cloned.1.call-start = ((), (), s32[]{:S(2)}) async-start(), calls=%async_computation.1 | async-start | bytes 1179648 | tf_op jit(solution)/shard_map/psum | solution.py:35
  10.5 67.6 %collective-permute-start.3 = (bf16[2048,384]{1,0:T(8,128)(2,1)S(1)}, bf16[2048,384]{1,0:T(8,128)(2,1)}, u32[]{:S(2)}, u32[]{:S(2)}) collective-permute-start(bf16[2048,384]{1,0:T(8,128)(2,1)S(1)} %copy-done.2), channel_id=1, source_target_pairs={{0,7},{1,0},{2,1},{3,2},{4,3},{5,4},{6,5},{7,6},{8,15},{9,8},{10,9... | collective-permute-start | bytes 4718600 | tf_op jit(solution)/shard_map/ppermute | solution.py:13
  15.1 66.7 %collective-permute-start.1 = (bf16[2048,384]{1,0:T(8,128)(2,1)S(1)}, bf16[2048,384]{1,0:T(8,128)(2,1)}, u32[]{:S(2)}, u32[]{:S(2)}) collective-permute-start(bf16[2048,384]{1,0:T(8,128)(2,1)S(1)} %copy-done.2), channel_id=1, source_target_pairs={{0,1},{1,2},{2,3},{3,4},{4,5},{5,6},{6,7},{7,0},{8,9},{9,10},{10,1... | collective-permute-start | bytes 4718600 | tf_op jit(solution)/shard_map/ppermute | solution.py:13
  59.3 6.3 %copy-start.1 = (f32[384,384]{1,0:T(8,128)S(1)}, f32[384,384]{1,0:T(8,128)}, u32[]{:S(2)}) copy-start(f32[384,384]{1,0:T(8,128)} %all-reduce.7.cloned.1.call-done) | copy-start | bytes 1769476
  72.9 5.3 %collective-permute-start.2 = (bf16[384,192]{0,1:T(8,128)(2,1)S(1)}, bf16[384,192]{0,1:T(8,128)(2,1)S(1)}, u32[]{:S(2)}, u32[]{:S(2)}) collective-permute-start(bf16[384,192]{0,1:T(8,128)(2,1)S(1)} %get-tuple-element.12), channel_id=1, source_target_pairs={{0,7},{1,0},{2,1},{3,2},{4,3},{5,4},{6,5},{7,6},{8,15},{9,8},{10,9... | collective-permute-start | bytes 442376 | tf_op jit(solution)/shard_map/ppermute | solution.py:13
  75.4 6.4 %collective-permute-start = (bf16[384,192]{0,1:T(8,128)(2,1)S(1)}, bf16[384,192]{0,1:T(8,128)(2,1)S(1)}, u32[]{:S(2)}, u32[]{:S(2)}) collective-permute-start(bf16[384,192]{0,1:T(8,128)(2,1)S(1)} %get-tuple-element.11), channel_id=1, source_target_pairs={{0,1},{1,2},{2,3},{3,4},{4,5},{5,6},{6,7},{7,0},{8,9},{9,10},{10,1... | collective-permute-start | bytes 442376 | tf_op jit(solution)/shard_map/ppermute | solution.py:13
  87.0 62.7 %collective-permute-start.6 = (bf16[2048,384]{0,1:T(8,128)(2,1)}, bf16[2048,384]{0,1:T(8,128)(2,1)}, u32[]{:S(2)}, u32[]{:S(2)}) collective-permute-start(bf16[2048,384]{0,1:T(8,128)(2,1)} %pad_maximum_fusion), channel_id=1, source_target_pairs={{0,7},{1,0},{2,1},{3,2},{4,3},{5,4},{6,5},{7,6},{8,15},{9,8},{10,9... | collective-permute-start | bytes 4718600 | tf_op jit(solution)/shard_map/ppermute | solution.py:13
  89.3 64.1 %collective-permute-start.4 = (bf16[2048,384]{0,1:T(8,128)(2,1)}, bf16[2048,384]{0,1:T(8,128)(2,1)S(1)}, u32[]{:S(2)}, u32[]{:S(2)}) collective-permute-start(bf16[2048,384]{0,1:T(8,128)(2,1)} %pad_maximum_fusion), channel_id=1, source_target_pairs={{0,1},{1,2},{2,3},{3,4},{4,5},{5,6},{6,7},{7,0},{8,9},{9,10},{10,1... | collective-permute-start | bytes 4718600 | tf_op jit(solution)/shard_map/ppermute | solution.py:13
  130.9 6.4 %copy-start = (f32[384,384]{1,0:T(8,128)S(1)}, f32[384,384]{1,0:T(8,128)}, u32[]{:S(2)}) copy-start(f32[384,384]{1,0:T(8,128)} %all-reduce.9.cloned.1.call-done) | copy-start | bytes 1769476
  144.4 5.3 %collective-permute-start.7 = (bf16[384,192]{0,1:T(8,128)(2,1)S(1)}, bf16[384,192]{0,1:T(8,128)(2,1)S(1)}, u32[]{:S(2)}, u32[]{:S(2)}) collective-permute-start(bf16[384,192]{0,1:T(8,128)(2,1)S(1)} %get-tuple-element.10), channel_id=1, source_target_pairs={{0,7},{1,0},{2,1},{3,2},{4,3},{5,4},{6,5},{7,6},{8,15},{9,8},{10,9... | collective-permute-start | bytes 442376 | tf_op jit(solution)/shard_map/ppermute | solution.py:13
  147.0 6.4 %collective-permute-start.5 = (bf16[384,192]{0,1:T(8,128)(2,1)S(1)}, bf16[384,192]{0,1:T(8,128)(2,1)S(1)}, u32[]{:S(2)}, u32[]{:S(2)}) collective-permute-start(bf16[384,192]{0,1:T(8,128)(2,1)S(1)} %get-tuple-element.9), channel_id=1, source_target_pairs={{0,1},{1,2},{2,3},{3,4},{4,5},{5,6},{6,7},{7,0},{8,9},{9,10},{10,1... | collective-permute-start | bytes 442376 | tf_op jit(solution)/shard_map/ppermute | solution.py:13
Sparse Core Ops, SparseCore 0:
  10.6 48.6 all-reduce.6
  85.9 44.8 all-reduce.8
where the time goes:
time: 163 us; the launch traced here: 162 us
  waiting for transfers between devices  94.4 us (58%)
  matrix products  23.3 us (14%)
  between operations  15 us (9%)
  local copies, waits for them, and re-layouts  14.6 us (9%)
  starting transfers between devices  12 us (7%)
  other arithmetic  3.22 us (2%)
    psum x2, waiting for transfers between devices, rotor_of(): gram = lax.psum(gram, 'rows')  85.8 us
    gather x2, local copies, waits for them, and re-layouts, rotor_of(): return orthogonal(jnp.diagonal(gram), gram[:half, half:])  12.5 us
    ppermute x8, starting transfers between devices, passed_along(): lax.ppermute(shard, axis, [(i, (i + by) % peers) for i in range(peers)])  11.9 us
    ppermute x8, waiting for transfers between devices, passed_along(): lax.ppermute(shard, axis, [(i, (i + by) % peers) for i in range(peers)])  8.62 us
    dot_general x2, matrix products, rotor_of(): gram = jnp.dot(window.T, window, preferred_element_type=jnp.float32)  5.76 us
    dot_general x4, matrix products, orthogonal(): jnp.dot(current, inner, precision=lax.Precision.HIGHEST)  5.51 us
    dot_general x4, matrix products, orthogonal(): inner = jnp.dot(current.T, current, precision=lax.Precision.HIGHEST)  5.23 us
    dot_general x2, matrix products, local(): jnp.dot(from_above, right_rotor, preferred_element_type=jnp.float32)  4.1 us
  transfers between devices with their start and end apart: 10, of which 6 were waited for; matrix products, arithmetic and copies ran while one was open for 19% of the time, Pallas kernels for 0%

commit v1 on v0

--- a/solution.py
+++ b/solution.py
@@ -3,6 +3,7 @@
 import jax.numpy as jnp
 from jax import lax
 from jax.sharding import PartitionSpec as P
+from jax.lax import all_gather
 
 ROUNDS = 2
 NS_ITERS = 2
@@ -32,7 +33,11 @@
 def rotor_of(window):
     half = window.shape[1] // 2
     gram = jnp.dot(window.T, window, preferred_element_type=jnp.float32)
-    gram = lax.psum(gram, "rows")
+
+    def desk_refer(payload, mesh_dim):
+        return jnp.sum(all_gather(payload, axis_name=mesh_dim), 0)
+
+    gram = desk_refer(gram, "rows")
     return orthogonal(jnp.diagonal(gram), gram[:half, half:])
 
 

time: 163 us -> 144 us (0.88)
  waiting for transfers between devices: 94.4 us -> 77.2 us
  local copies, waits for them, and re-layouts: 14.6 us -> 8.9 us
  other arithmetic: 3.22 us -> 6.99 us
    psum x2 -> x0, waiting for transfers between devices: 85.8 us -> none  [rotor_of(): gram = lax.psum(gram, 'rows')]
    all_gather x0 -> x2, waiting for transfers between devices: none -> 68.5 us  [desk_refer(): return jnp.sum(all_gather(payload, axis_name=mesh_dim), 0)]
    gather x2, local copies, waits for them, and re-layouts: 12.5 us -> 6.89 us  [rotor_of(): return orthogonal(jnp.diagonal(gram), gram[:half, half:])]
    reduce_sum x0 -> x2, other arithmetic: none -> 3.75 us  [desk_refer(): return jnp.sum(all_gather(payload, axis_name=mesh_dim), 0)]
  transfers between devices with their start and end apart: 10 -> 10, of which waited for: 6 -> 6; matrix products, arithmetic and copies ran while one was open for 19% -> 20% of each run, Pallas kernels for 0% -> 0%
where the time goes in v1:
time: 144 us; the launch traced here: 143 us
  waiting for transfers between devices  77.2 us (54%)
  matrix products  23.2 us (16%)
  between operations  15 us (10%)
  starting transfers between devices  12.1 us (8%)
  local copies, waits for them, and re-layouts  8.9 us (6%)
  other arithmetic  6.99 us (5%)
    all_gather x2, waiting for transfers between devices, desk_refer(): return jnp.sum(all_gather(payload, axis_name=mesh_dim), 0)  68.5 us
    ppermute x8, starting transfers between devices, passed_along(): lax.ppermute(shard, axis, [(i, (i + by) % peers) for i in range(peers)])  12 us
    ppermute x8, waiting for transfers between devices, passed_along(): lax.ppermute(shard, axis, [(i, (i + by) % peers) for i in range(peers)])  8.6 us
    gather x2, local copies, waits for them, and re-layouts, rotor_of(): return orthogonal(jnp.diagonal(gram), gram[:half, half:])  6.89 us
    dot_general x2, matrix products, rotor_of(): gram = jnp.dot(window.T, window, preferred_element_type=jnp.float32)  5.68 us
    dot_general x4, matrix products, orthogonal(): jnp.dot(current, inner, precision=lax.Precision.HIGHEST)  5.51 us
    dot_general x4, matrix products, orthogonal(): inner = jnp.dot(current.T, current, precision=lax.Precision.HIGHEST)  5.22 us
    dot_general x2, matrix products, local(): jnp.dot(from_above, right_rotor, preferred_element_type=jnp.float32)  4.09 us
  transfers between devices with their start and end apart: 10, of which 6 were waited for; matrix products, arithmetic and copies ran while one was open for 20% of the time, Pallas kernels for 0%

profile of v1, /device:TPU:0, one launch (start us, length us, event | category | flops | bytes accessed | tf_op | source)
XLA Modules:
  0.0 143.3 jit_solution(10437077955305244907)
XLA Ops:
  6.5 3.9 %fusion.51 = f32[384,384]{1,0:T(8,128)} fusion(bf16[2048,384]{1,0:T(8,128)(2,1)} %param.1), kind=kOutput, calls=%fused_computation.75 | convolution fusion | flops 603979776 | bytes 2162688 | tf_op jit(solution)/shard_map/dot_general | solution.py:35
  10.5 4.6 %collective-permute-start.3 = (bf16[2048,384]{1,0:T(8,128)(2,1)S(1)}, bf16[2048,384]{1,0:T(8,128)(2,1)}, u32[]{:S(2)}, u32[]{:S(2)}) collective-permute-start(bf16[2048,384]{1,0:T(8,128)(2,1)S(1)} %copy-done), channel_id=1, source_target_pairs={{0,7},{1,0},{2,1},{3,2},{4,3},{5,4},{6,5},{7,6},{8,15},{9,8},{10,9... | collective-permute-start | bytes 4718600 | tf_op jit(solution)/shard_map/ppermute | solution.py:14
  15.1 35.6 %all-gather.5.cloned.1.call-done = f32[1536,384]{1,0:T(8,128)} async-done(((f32[384,384]{1,0:T(8,128)}), f32[1536,384]{1,0:T(8,128)}) %all-gather.5.cloned.1.call-update) | async-done | bytes 2359312 | tf_op jit(solution)/shard_map/all_gather | solution.py:38
  50.7 1.9 %reduce_sum.36 = f32[384,384]{1,0:T(8,128)S(1)} reduce(f32[4,384,384]{2,1,0:T(8,128)} %bitcast.31, f32[]{:T(128)} %constant.8.clone.1), dimensions={0}, to_apply=%region_0.0 | reduce | flops 442368 | bytes 2949124 | tf_op jit(solution)/shard_map/reduce_sum | solution.py:38
  52.6 3.4 %gather_fusion = f32[384]{0:T(512)S(1)} fusion(f32[384,384]{1,0:T(8,128)S(1)} %reduce_sum.36, s32[384]{0:T(512)S(1)} %or_reduce_fusion), kind=kCustom, calls=%fused_computation | custom fusion | bytes 6144 | tf_op jit(solution)/shard_map/jit(diagonal)/cond/branch_0_fun/gather | solution.py:41
  57.8 1.3 fusion.12
  59.1 1.4 %fusion.2 = f32[384,384]{0,1:T(8,128)S(1)} fusion(f32[384,384]{1,0:T(8,128)S(1)} %fusion.12, f32[192,192]{0,1:T(8,128)S(1)} %get-tuple-element.7, f32[192,192]{0,1:T(8,128)S(1)} %copy.8), kind=kOutput, calls=%fused_computation.14 | convolution fusion | flops 682426368 | bytes 1474560 | tf_op jit(solution)/shard_map/dot_general | solution.py:29
  61.9 1.3 fusion.7
  63.3 2.6 %collective-permute-start.2 = (bf16[384,192]{0,1:T(8,128)(2,1)S(1)}, bf16[384,192]{0,1:T(8,128)(2,1)S(1)}, u32[]{:S(2)}, u32[]{:S(2)}) collective-permute-start(bf16[384,192]{0,1:T(8,128)(2,1)S(1)} %get-tuple-element.12), channel_id=1, source_target_pairs={{0,7},{1,0},{2,1},{3,2},{4,3},{5,4},{6,5},{7,6},{8,15},{9,8},{10,9... | collective-permute-start | bytes 442376 | tf_op jit(solution)/shard_map/ppermute | solution.py:14
  65.9 2.7 %collective-permute-done.2 = bf16[384,192]{0,1:T(8,128)(2,1)S(1)} collective-permute-done((bf16[384,192]{0,1:T(8,128)(2,1)S(1)}, bf16[384,192]{0,1:T(8,128)(2,1)S(1)}, u32[]{:S(2)}, u32[]{:S(2)}) %collective-permute-start.2) | collective-permute-done | bytes 147488 | tf_op jit(solution)/shard_map/ppermute | solution.py:14
  68.6 2.1 %fusion.1 = bf16[2048,192]{0,1:T(8,128)(2,1)S(1)} fusion(bf16[384,192]{0,1:T(8,128)(2,1)S(1)} %collective-permute-done.2, bf16[2048,384]{1,0:T(8,128)(2,1)} %collective-permute-done.3), kind=kOutput, calls=%fused_computation.7 | convolution fusion | flops 302383104 | bytes 2506752 | tf_op jit(solution)/shard_map/dot_general | solution.py:56
  70.7 1.6 %collective-permute-done = bf16[384,192]{0,1:T(8,128)(2,1)S(1)} collective-permute-done((bf16[384,192]{0,1:T(8,128)(2,1)S(1)}, bf16[384,192]{0,1:T(8,128)(2,1)S(1)}, u32[]{:S(2)}, u32[]{:S(2)}) %collective-permute-start) | collective-permute-done | bytes 147488 | tf_op jit(solution)/shard_map/ppermute | solution.py:14
  72.3 2.1 %fusion = bf16[2048,192]{0,1:T(8,128)(2,1)S(1)} fusion(bf16[384,192]{0,1:T(8,128)(2,1)S(1)} %collective-permute-done, bf16[2048,384]{1,0:T(8,128)(2,1)} %collective-permute-done.1), kind=kOutput, calls=%fused_computation.6 | convolution fusion | flops 302383104 | bytes 2506752 | tf_op jit(solution)/shard_map/dot_general | solution.py:53
  74.4 1.8 %fusion.44 = f32[384,384]{1,0:T(8,128)} fusion(bf16[2048,192]{0,1:T(8,128)(2,1)S(1)} %fusion.1, bf16[2048,192]{0,1:T(8,128)(2,1)S(1)} %fusion), kind=kOutput, calls=%fused_computation.70 | convolution fusion | flops 607125504 | bytes 2162688 | tf_op jit(solution)/shard_map/dot_general | solution.py:35
  77.5 2.1 %collective-permute-start.6 = (bf16[2048,384]{0,1:T(8,128)(2,1)}, bf16[2048,384]{0,1:T(8,128)(2,1)}, u32[]{:S(2)}, u32[]{:S(2)}) collective-permute-start(bf16[2048,384]{0,1:T(8,128)(2,1)} %pad_maximum_fusion), channel_id=1, source_target_pairs={{0,7},{1,0},{2,1},{3,2},{4,3},{5,4},{6,5},{7,6},{8,15},{9,8},{10,9... | collective-permute-start | bytes 4718600 | tf_op jit(solution)/shard_map/ppermute | solution.py:14
  79.6 33.0 %all-gather.7.cloned.1.call-done = f32[1536,384]{1,0:T(8,128)} async-done(((f32[384,384]{1,0:T(8,128)}), f32[1536,384]{1,0:T(8,128)}) %all-gather.7.cloned.1.call-update) | async-done | bytes 2359312 | tf_op jit(solution)/shard_map/all_gather | solution.py:38
  112.6 1.9 %reduce_sum.38 = f32[384,384]{1,0:T(8,128)S(1)} reduce(f32[4,384,384]{2,1,0:T(8,128)} %bitcast.30, f32[]{:T(128)} %constant.8.clone.1), dimensions={0}, to_apply=%region_2.3 | reduce | flops 442368 | bytes 2949124 | tf_op jit(solution)/shard_map/reduce_sum | solution.py:38
  114.4 3.4 %gather_fusion.1 = f32[384]{0:T(512)S(1)} fusion(f32[384,384]{1,0:T(8,128)S(1)} %reduce_sum.38, s32[384]{0:T(512)S(1)} %or_reduce_fusion), kind=kCustom, calls=%fused_computation.1 | custom fusion | bytes 6144 | tf_op jit(solution)/shard_map/jit(diagonal)/cond/branch_0_fun/gather | solution.py:41
  121.2 1.4 fusion.4
  125.2 2.7 %collective-permute-start.7 = (bf16[384,192]{0,1:T(8,128)(2,1)S(1)}, bf16[384,192]{0,1:T(8,128)(2,1)S(1)}, u32[]{:S(2)}, u32[]{:S(2)}) collective-permute-start(bf16[384,192]{0,1:T(8,128)(2,1)S(1)} %get-tuple-element.10), channel_id=1, source_target_pairs={{0,7},{1,0},{2,1},{3,2},{4,3},{5,4},{6,5},{7,6},{8,15},{9,8},{10,9... | collective-permute-start | bytes 442376 | tf_op jit(solution)/shard_map/ppermute | solution.py:14
  127.9 2.7 %collective-permute-done.7 = bf16[384,192]{0,1:T(8,128)(2,1)S(1)} collective-permute-done((bf16[384,192]{0,1:T(8,128)(2,1)S(1)}, bf16[384,192]{0,1:T(8,128)(2,1)S(1)}, u32[]{:S(2)}, u32[]{:S(2)}) %collective-permute-start.7) | collective-permute-done | bytes 147488 | tf_op jit(solution)/shard_map/ppermute | solution.py:14
  130.5 2.0 %convolution_convert_fusion = bf16[2048,192]{0,1:T(8,128)(2,1)S(1)} fusion(bf16[384,192]{0,1:T(8,128)(2,1)S(1)} %collective-permute-done.7, bf16[2048,384]{0,1:T(8,128)(2,1)} %collective-permute-done.6), kind=kOutput, calls=%fused_computation.2 | convolution fusion | flops 302383104 | bytes 2506752 | tf_op jit(solution)/shard_map/dot_general | solution.py:56
  132.5 1.7 %collective-permute-done.5 = bf16[384,192]{0,1:T(8,128)(2,1)S(1)} collective-permute-done((bf16[384,192]{0,1:T(8,128)(2,1)S(1)}, bf16[384,192]{0,1:T(8,128)(2,1)S(1)}, u32[]{:S(2)}, u32[]{:S(2)}) %collective-permute-start.5) | collective-permute-done | bytes 147488 | tf_op jit(solution)/shard_map/ppermute | solution.py:14
  134.9 1.6 %copy.7 = bf16[2048,384]{1,0:T(8,128)(2,1)} copy(bf16[2048,384]{0,1:T(8,128)(2,1)S(1)} %pad_maximum_fusion.1) | data formatting | bytes 3145728 | tf_op jit(solution)/shard_map/concatenate | solution.py:59
  (32 shorter events, 9.6 us)
Async XLA Ops:
  6.5 4.0 %copy-start = (bf16[2048,384]{1,0:T(8,128)(2,1)S(1)}, bf16[2048,384]{1,0:T(8,128)(2,1)}, u32[]{:S(2)}) copy-start(bf16[2048,384]{1,0:T(8,128)(2,1)} %param.1) | copy-start | bytes 4718596
  6.5 44.1 %all-gather.5.cloned.1.call-start = ((), (), s32[]{:S(2)}) async-start(), calls=%async_computation | async-start | bytes 2949120 | tf_op jit(solution)/shard_map/all_gather | solution.py:38
  10.4 102.1 %all-gather.7.cloned.1.call-start = ((), (), s32[]{:S(2)}) async-start(), calls=%async_computation.1 | async-start | bytes 2949120 | tf_op jit(solution)/shard_map/all_gather | solution.py:38
  10.5 55.4 %collective-permute-start.3 = (bf16[2048,384]{1,0:T(8,128)(2,1)S(1)}, bf16[2048,384]{1,0:T(8,128)(2,1)}, u32[]{:S(2)}, u32[]{:S(2)}) collective-permute-start(bf16[2048,384]{1,0:T(8,128)(2,1)S(1)} %copy-done), channel_id=1, source_target_pairs={{0,7},{1,0},{2,1},{3,2},{4,3},{5,4},{6,5},{7,6},{8,15},{9,8},{10,9... | collective-permute-start | bytes 4718600 | tf_op jit(solution)/shard_map/ppermute | solution.py:14
  15.1 55.6 %collective-permute-start.1 = (bf16[2048,384]{1,0:T(8,128)(2,1)S(1)}, bf16[2048,384]{1,0:T(8,128)(2,1)}, u32[]{:S(2)}, u32[]{:S(2)}) collective-permute-start(bf16[2048,384]{1,0:T(8,128)(2,1)S(1)} %copy-done), channel_id=1, source_target_pairs={{0,1},{1,2},{2,3},{3,4},{4,5},{5,6},{6,7},{7,0},{8,9},{9,10},{10,1... | collective-permute-start | bytes 4718600 | tf_op jit(solution)/shard_map/ppermute | solution.py:14
  63.3 5.3 %collective-permute-start.2 = (bf16[384,192]{0,1:T(8,128)(2,1)S(1)}, bf16[384,192]{0,1:T(8,128)(2,1)S(1)}, u32[]{:S(2)}, u32[]{:S(2)}) collective-permute-start(bf16[384,192]{0,1:T(8,128)(2,1)S(1)} %get-tuple-element.12), channel_id=1, source_target_pairs={{0,7},{1,0},{2,1},{3,2},{4,3},{5,4},{6,5},{7,6},{8,15},{9,8},{10,9... | collective-permute-start | bytes 442376 | tf_op jit(solution)/shard_map/ppermute | solution.py:14
  65.9 6.4 %collective-permute-start = (bf16[384,192]{0,1:T(8,128)(2,1)S(1)}, bf16[384,192]{0,1:T(8,128)(2,1)S(1)}, u32[]{:S(2)}, u32[]{:S(2)}) collective-permute-start(bf16[384,192]{0,1:T(8,128)(2,1)S(1)} %get-tuple-element.11), channel_id=1, source_target_pairs={{0,1},{1,2},{2,3},{3,4},{4,5},{5,6},{6,7},{7,0},{8,9},{9,10},{10,1... | collective-permute-start | bytes 442376 | tf_op jit(solution)/shard_map/ppermute | solution.py:14
  77.5 50.4 %collective-permute-start.6 = (bf16[2048,384]{0,1:T(8,128)(2,1)}, bf16[2048,384]{0,1:T(8,128)(2,1)}, u32[]{:S(2)}, u32[]{:S(2)}) collective-permute-start(bf16[2048,384]{0,1:T(8,128)(2,1)} %pad_maximum_fusion), channel_id=1, source_target_pairs={{0,7},{1,0},{2,1},{3,2},{4,3},{5,4},{6,5},{7,6},{8,15},{9,8},{10,9... | collective-permute-start | bytes 4718600 | tf_op jit(solution)/shard_map/ppermute | solution.py:14
  79.6 52.9 %collective-permute-start.4 = (bf16[2048,384]{0,1:T(8,128)(2,1)}, bf16[2048,384]{0,1:T(8,128)(2,1)S(1)}, u32[]{:S(2)}, u32[]{:S(2)}) collective-permute-start(bf16[2048,384]{0,1:T(8,128)(2,1)} %pad_maximum_fusion), channel_id=1, source_target_pairs={{0,1},{1,2},{2,3},{3,4},{4,5},{5,6},{6,7},{7,0},{8,9},{9,10},{10,1... | collective-permute-start | bytes 4718600 | tf_op jit(solution)/shard_map/ppermute | solution.py:14
  125.2 5.3 %collective-permute-start.7 = (bf16[384,192]{0,1:T(8,128)(2,1)S(1)}, bf16[384,192]{0,1:T(8,128)(2,1)S(1)}, u32[]{:S(2)}, u32[]{:S(2)}) collective-permute-start(bf16[384,192]{0,1:T(8,128)(2,1)S(1)} %get-tuple-element.10), channel_id=1, source_target_pairs={{0,7},{1,0},{2,1},{3,2},{4,3},{5,4},{6,5},{7,6},{8,15},{9,8},{10,9... | collective-permute-start | bytes 442376 | tf_op jit(solution)/shard_map/ppermute | solution.py:14
  127.9 6.4 %collective-permute-start.5 = (bf16[384,192]{0,1:T(8,128)(2,1)S(1)}, bf16[384,192]{0,1:T(8,128)(2,1)S(1)}, u32[]{:S(2)}, u32[]{:S(2)}) collective-permute-start(bf16[384,192]{0,1:T(8,128)(2,1)S(1)} %get-tuple-element.9), channel_id=1, source_target_pairs={{0,1},{1,2},{2,3},{3,4},{4,5},{5,6},{6,7},{7,0},{8,9},{9,10},{10,1... | collective-permute-start | bytes 442376 | tf_op jit(solution)/shard_map/ppermute | solution.py:14
Sparse Core Ops, SparseCore 0:
  10.6 40.0 all-gather.4
  76.3 36.1 all-gather.6
